TPU v7x, 32 devices: a whole 2x2x4 slice. The times are simulated.
32 devices in a mesh: fsdp: 4 (over z), adapter: 8 (over y, x, core).
Axes of the slice: x: 2, y: 2, z: 4, core: 2. Of those that a mesh axis runs over, the one named last changes fastest.
Arguments:
- tokens: bfloat16 [2048, 8192], P('adapter', 'fsdp'), may hold values from -6 to 6
- tenant: int32 [2048], P('adapter'), may hold values from 0 to 63, as said below
- send_list: int32 [8, 8, 128], P('adapter'), may hold values from -1 to 255, as said below
- base_weight: bfloat16 [8192, 2048], P('fsdp'), may hold values from -0.09375 to 0.09375
- down_weight: bfloat16 [64, 8192, 128], P('adapter', 'fsdp'), may hold values from -0.0625 to 0.0625
- up_projection_weight: bfloat16 [64, 64, 2048], P('adapter', None, 'fsdp'), may hold values from -0.75 to 0.75
- cotangent: bfloat16 [2048, 2048], P('adapter', 'fsdp'), may hold values from -3 to 3
Outputs:
- projected: bfloat16 [2048, 2048], P('adapter', 'fsdp')
- token_gradient: bfloat16 [2048, 8192], P('adapter', 'fsdp')
- down_weight_gradient: bfloat16 [64, 8192, 128], P('adapter', 'fsdp')
- up_weight_gradient: bfloat16 [64, 64, 2048], P('adapter', None, 'fsdp')
Inputs may be any that keep to these rules, and one draw needn't show every extreme that they name: `tenant`: adapter t belongs to owner t // 8. Among the 256 rows of one index of adapter at most 128 belong to the adapters of one owner, and one owner, the same for every index, has exactly 128 of them. send_list[i, o, :] lists in increasing order the rows (numbered within the 256 rows of index i of adapter) whose tenant belongs to owner o, then -1 in the slots left; every row stands in exactly one list.
All inputs are finite; a program needn't handle non-finite values.
Results may differ from a plain program's by a relative error of at most 0.005.
Values may be sent and summed in bfloat16 or wider, within the bound.
No kernel may reach another device: no remote copies, remote signals or barrier semaphores. Data moves between devices by JAX's collectives and lax.ppermute only.
A program may use at most 128 MiB of HBM per device.

v0:
```python
import jax
import jax.numpy as jnp
from jax import lax
from jax.sharding import PartitionSpec as P

KV = 1024
adapter_scale = 0.5


def down_partial(input_rows, weights_f, down_weight):
    low_all = jnp.einsum("sd,ldk->slk", input_rows, down_weight, preferred_element_type=jnp.float32)
    return jnp.sum(low_all * weights_f[:, :, None], axis=1)


def grad_partial(rows_dy, weights_f, up_projection_weight, selected_half):
    rank_size = up_projection_weight.shape[1]
    back_all = jnp.einsum(
        "sc,lrc->slr", rows_dy, up_projection_weight, preferred_element_type=jnp.float32
    )
    half_sum = jnp.sum(back_all * weights_f[:, :, None], axis=1)
    placed = jnp.zeros((rows_dy.shape[0], 2 * rank_size), jnp.float32)
    zero_idx = jnp.zeros((), jnp.int32)
    return lax.dynamic_update_slice(placed, half_sum, (zero_idx, selected_half * rank_size))


def forward_holder(low_rank, weight_table, up_projection_weight, selected_half):
    rank_size = up_projection_weight.shape[1]
    low_half = lax.dynamic_slice_in_dim(low_rank, selected_half * rank_size, rank_size, 1)
    broadcast_rows = low_half[:, None, :] * weight_table[:, :, None]
    adapter_update = adapter_scale * jnp.einsum(
        "slr,lrc->sc", broadcast_rows, up_projection_weight, preferred_element_type=jnp.float32
    )
    return (adapter_update.astype(jnp.bfloat16), broadcast_rows)


def backward_owner(back_low, weight_table, input_rows, rows_dy, broadcast_rows, down_weight):
    widened_rows = back_low[:, None, :] * weight_table[:, :, None]
    backward_update = adapter_scale * jnp.einsum(
        "wnr,nyr->wy", widened_rows, down_weight, preferred_element_type=jnp.float32
    )
    down_weight_gradient = adapter_scale * jnp.einsum(
        "wq,wmu->mqu", input_rows, widened_rows, preferred_element_type=jnp.float32
    )
    up_weight_gradient = adapter_scale * jnp.einsum(
        "slr,sc->lrc", broadcast_rows, rows_dy, preferred_element_type=jnp.float32
    )
    return (
        backward_update.astype(jnp.bfloat16),
        down_weight_gradient.astype(jnp.bfloat16),
        up_weight_gradient.astype(jnp.bfloat16),
    )


def shards(tokens, tenant, send_list, base_weight, down_weight, up_projection_weight, cotangent):
    rows_here = tokens.shape[0]
    width_here = tokens.shape[1]
    column_span = cotangent.shape[1]
    adapters_here = down_weight.shape[0]
    holder_list = send_list.shape[1]
    slot_capacity = send_list.shape[2]
    total_slots = holder_list * slot_capacity
    listed = send_list[0]
    present = listed >= 0
    safe_rows = jnp.where(present, listed, 0)
    local_ids = tenant % adapters_here
    picked_ids = local_ids[safe_rows]
    adapter_ids = jnp.arange(adapters_here, dtype=jnp.int32)
    selector = (
        (picked_ids[:, :, None] == adapter_ids[None, None, :]) & present[:, :, None]
    ).astype(jnp.bfloat16)
    send_x = tokens[safe_rows]
    send_dy = cotangent[safe_rows]
    drop_rows = jnp.where(present, listed, rows_here).reshape(total_slots)
    fsdp_pos = lax.axis_index("fsdp")
    selected_half = fsdp_pos * column_span // KV
    weight_cols = base_weight
    local_base_output = lax.psum_scatter(
        lax.dot_general(
            weight_cols, tokens, (((0,), (1,)), ((), ())), preferred_element_type=jnp.float32
        ),
        "fsdp",
        scatter_dimension=0,
        tiled=True,
    ).T
    weight_cols = base_weight
    input_frozen_part = lax.dot_general(
        lax.all_gather(cotangent, "fsdp", axis=1, tiled=True),
        weight_cols,
        (((1,), (1,)), ((), ())),
        preferred_element_type=jnp.float32,
    )
    recv_x, recv_sel = (
        lax.all_to_all(send_x, "adapter", split_axis=0, concat_axis=0, tiled=True),
        lax.all_to_all(selector, "adapter", split_axis=0, concat_axis=0, tiled=True),
    )
    input_rows = recv_x.reshape(total_slots, width_here)
    weight_table = recv_sel.reshape(total_slots, adapters_here)
    weights_f = weight_table.astype(jnp.float32)
    low_term = down_partial(input_rows, weights_f, down_weight)
    reduced_rank_sum = lax.psum(low_term, "fsdp")
    adapter_update, broadcast_rows = forward_holder(
        reduced_rank_sum.astype(jnp.bfloat16), weight_table, up_projection_weight, selected_half
    )
    got_delta = lax.all_to_all(
        adapter_update.reshape(holder_list, slot_capacity, column_span),
        "adapter",
        split_axis=0,
        concat_axis=0,
        tiled=True,
    )
    recv_dy = lax.all_to_all(send_dy, "adapter", split_axis=0, concat_axis=0, tiled=True)
    rows_dy = recv_dy.reshape(total_slots, column_span)
    back_sum = lax.psum(
        grad_partial(rows_dy, weights_f, up_projection_weight, selected_half), "fsdp"
    )
    backward_update, down_weight_gradient, up_weight_gradient = backward_owner(
        back_sum.astype(jnp.bfloat16),
        weight_table,
        input_rows,
        rows_dy,
        broadcast_rows,
        down_weight,
    )
    got_back = lax.all_to_all(
        backward_update.reshape(holder_list, slot_capacity, width_here),
        "adapter",
        split_axis=0,
        concat_axis=0,
        tiled=True,
    )
    adapter_columns = (
        jnp.zeros((rows_here, column_span), jnp.float32)
        .at[drop_rows]
        .add(got_delta.reshape(total_slots, column_span).astype(jnp.float32), mode="drop")
    )
    projected = (local_base_output + adapter_columns).astype(jnp.bfloat16)
    adapter_backward = (
        jnp.zeros((rows_here, width_here), jnp.float32)
        .at[drop_rows]
        .add(got_back.reshape(total_slots, width_here).astype(jnp.float32), mode="drop")
    )
    token_gradient = (input_frozen_part + adapter_backward).astype(jnp.bfloat16)
    return (projected, token_gradient, down_weight_gradient, up_weight_gradient)


def solution(mesh):
    in_specs = (
        P("adapter", "fsdp"),
        P("adapter"),
        P("adapter", None, None),
        P("fsdp", None),
        P("adapter", "fsdp", None),
        P("adapter", None, "fsdp"),
        P("adapter", "fsdp"),
    )
    out_specs = (
        P("adapter", "fsdp"),
        P("adapter", "fsdp"),
        P("adapter", "fsdp", None),
        P("adapter", None, "fsdp"),
    )
    return jax.shard_map(shards, mesh=mesh, in_specs=in_specs, out_specs=out_specs, check_vma=False)
```

profile of v0, /device:TPU:0, one launch (start us, length us, event | category | flops | bytes accessed | tf_op | source)
XLA Modules:
  0.0 267.3 jit_solution(12076343468223439721)
XLA Ops:
  7.2 0.8 fusion.29
  8.0 0.7 compare_bitcast_fusion
  8.7 0.7 and_select_fusion
  9.4 6.8 %gather_fusion.1 = s32[1024]{0:T(1024)S(1)} fusion(s32[256]{0:T(256)S(1)} %and_select_fusion, s32[1024]{0:T(1024)S(1)} %fusion.29), kind=kCustom, calls=%fused_computation.1 | custom fusion | bytes 12288 | tf_op jit(solution)/shard_map/gather | solution.py:66
  16.2 0.6 fusion.27
  16.8 5.2 %all-to-all-start.1 = ((bf16[8,128,8]{1,2,0:T(8,128)(2,1)}), bf16[8,128,8]{1,2,0:T(8,128)(2,1)S(1)}, u32[]{:S(2)}, u32[]{:S(2)}) async-start(bf16[8,128,8]{1,2,0:T(8,128)(2,1)} %fusion.27), calls=%async_computation.2 | async-start | bytes 32768 | tf_op jit(solution)/shard_map/all_to_all | solution.py:94
  22.0 5.1 %gather_fusion.2 = bf16[1024,512]{1,0:T(8,128)(2,1)} fusion(bf16[256,512]{1,0:T(8,128)(2,1)S(1)} %copy-done.1, s32[1024]{0:T(1024)S(1)} %fusion.29), kind=kCustom, calls=%fused_computation.2 | custom fusion | bytes 2101248 | tf_op jit(solution)/shard_map/gather | solution.py:72
  27.1 4.2 %all-to-all-start.3 = ((bf16[8,128,512]{2,1,0:T(8,128)(2,1)}), bf16[8,128,512]{2,1,0:T(8,128)(2,1)S(1)}, u32[]{:S(2)}, u32[]{:S(2)}) async-start(bf16[8,128,512]{2,1,0:T(8,128)(2,1)} %bitcast.14), calls=%async_computation.4 | async-start | bytes 2097152 | tf_op jit(solution)/shard_map/all_to_all | solution.py:111
  31.3 6.0 %gather_fusion = bf16[1024,2048]{1,0:T(8,128)(2,1)} fusion(bf16[256,2048]{1,0:T(8,128)(2,1)S(1)} %copy-done, s32[1024]{0:T(1024)S(1)} %fusion.29), kind=kCustom, calls=%fused_computation | custom fusion | bytes 8392704 | tf_op jit(solution)/shard_map/gather | solution.py:71
  37.2 9.4 %all-to-all-done.3 = bf16[8,128,512]{2,1,0:T(8,128)(2,1)S(1)} async-done(((bf16[8,128,512]{2,1,0:T(8,128)(2,1)}), bf16[8,128,512]{2,1,0:T(8,128)(2,1)S(1)}, u32[]{:S(2)}, u32[]{:S(2)}) %all-to-all-start.3) | async-done | bytes 1048608 | tf_op jit(solution)/shard_map/all_to_all | solution.py:111
  46.7 4.6 %all-to-all-start = ((bf16[8,128,2048]{2,1,0:T(8,128)(2,1)}), bf16[8,128,2048]{2,1,0:T(8,128)(2,1)}, u32[]{:S(2)}, u32[]{:S(2)}) async-start(bf16[8,128,2048]{2,1,0:T(8,128)(2,1)} %bitcast.50), calls=%async_computation.1 | async-start | bytes 8388608 | tf_op jit(solution)/shard_map/all_to_all | solution.py:93
  51.3 0.7 all-gather.2.cloned.1.call-update
  52.1 7.2 %fusion.31 = f32[2048,256]{1,0:T(8,128)} fusion(bf16[2048,2048]{1,0:T(8,128)(2,1)} %param.10, bf16[256,2048]{1,0:T(8,128)(2,1)S(1)} %copy-done), kind=kOutput, calls=%fused_computation.49 | convolution fusion | flops 2147483648 | bytes 11534336 | tf_op jit(solution)/shard_map/dot_general | solution.py:78
  59.4 0.7 multiply_reduce_fusion.1
  60.2 40.2 %all-to-all-done = bf16[8,128,2048]{2,1,0:T(8,128)(2,1)} async-done(((bf16[8,128,2048]{2,1,0:T(8,128)(2,1)}), bf16[8,128,2048]{2,1,0:T(8,128)(2,1)}, u32[]{:S(2)}, u32[]{:S(2)}) %all-to-all-start) | async-done | bytes 4194336 | tf_op jit(solution)/shard_map/all_to_all | solution.py:93
  100.4 7.6 %multiply_reduce_fusion = f32[1024,128]{1,0:T(8,128)S(1)} fusion(bf16[1024,2048,1]{1,0,2:T(8,128)(2,1)} %bitcast.7, bf16[8,2048,128]{2,1,0:T(8,128)(2,1)} %param.11, f32[1024,8]{0,1:T(8,128)S(1)} %bitcast_convert_fusion), kind=kOutput, calls=%fused_computation.10 | convolution fusion | flops 4296933376 | bytes 8945664 | tf_op jit(solution)/shard_map/sd,ldk->slk/dot_general | solution.py:11
  107.9 56.5 %all-reduce.2 = (bf16[1024,128]{1,0:T(8,128)(2,1)S(1)}, bf16[1024,128]{0,1:T(8,128)(2,1)}) all-reduce(f32[1024,128]{1,0:T(8,128)S(1)} %multiply_reduce_fusion, f32[1024,128]{0,1:T(8,128)S(1)} %constant_dynamic-update-slice_fusion), channel_id=1, replica_groups=mesh['fsdp'=4,'adapter'=8] {'fsdp'}, use_global_device_ids=true, to_apply=%region_2.3 | all-reduce | flops 262144 | bytes 1572864 | tf_op jit(solution)/shard_map/psum | solution.py:100
  164.7 2.8 %fusion.8 = bf16[1024,512]{1,0:T(8,128)(2,1)} fusion(bf16[8,64,512]{2,1,0:T(8,128)(2,1)} %param.12, bf16[1024,8]{0,1:T(8,128)(2,1)S(1)} %bitcast.57, bf16[1024,64]{0,1:T(8,128)(2,1)S(1)} %copy.17), kind=kOutput, calls=%fused_computation.17 | convolution fusion | flops 538443776 | bytes 1720320 | tf_op jit(solution)/shard_map/slr,lrc->sc/dot_general | solution.py:30
  167.4 3.6 %all-to-all-start.2 = ((bf16[8,128,512]{2,1,0:T(8,128)(2,1)}), bf16[8,128,512]{2,1,0:T(8,128)(2,1)S(1)}, u32[]{:S(2)}, u32[]{:S(2)}) async-start(bf16[8,128,512]{2,1,0:T(8,128)(2,1)} %bitcast.55), calls=%async_computation.3 | async-start | bytes 2097152 | tf_op jit(solution)/shard_map/all_to_all | solution.py:104
  171.0 8.4 %fusion.2 = bf16[1024,2048]{1,0:T(8,128)(2,1)} fusion(bf16[8,2048,128]{2,1,0:T(8,128)(2,1)} %param.11, bf16[1024,8]{0,1:T(8,128)(2,1)S(1)} %bitcast.58, bf16[1024,128]{0,1:T(8,128)(2,1)} %get-tuple-element.17), kind=kOutput, calls=%fused_computation.8 | convolution fusion | flops 4300210176 | bytes 8667136 | tf_op jit(solution)/shard_map/wnr,nyr->wy/dot_general | solution.py:38
  179.4 7.0 %all-to-all-done.2 = bf16[8,128,512]{2,1,0:T(8,128)(2,1)S(1)} async-done(((bf16[8,128,512]{2,1,0:T(8,128)(2,1)}), bf16[8,128,512]{2,1,0:T(8,128)(2,1)S(1)}, u32[]{:S(2)}, u32[]{:S(2)}) %all-to-all-start.2) | async-done | bytes 1048608 | tf_op jit(solution)/shard_map/all_to_all | solution.py:104
  186.5 4.9 %all-to-all-start.4 = ((bf16[8,128,2048]{2,1,0:T(8,128)(2,1)}), bf16[8,128,2048]{2,1,0:T(8,128)(2,1)}, u32[]{:S(2)}, u32[]{:S(2)}) async-start(bf16[8,128,2048]{2,1,0:T(8,128)(2,1)} %bitcast.51), calls=%async_computation.5 | async-start | bytes 8388608 | tf_op jit(solution)/shard_map/all_to_all | solution.py:124
  191.4 7.4 %fusion.32 = f32[256,2048]{1,0:T(8,128)} fusion(bf16[256,2048]{1,0:T(8,128)(2,1)} %all-gather.2.cloned.1.call-done, bf16[2048,2048]{1,0:T(8,128)(2,1)} %param.10), kind=kOutput, calls=%fused_computation.50 | convolution fusion | flops 2147483648 | bytes 11534336 | tf_op jit(solution)/shard_map/dot_general | solution.py:86
  198.8 8.2 %fusion.3 = bf16[8,2048,128]{1,2,0:T(8,128)(2,1)} fusion(bf16[1024,2048,1]{1,0,2:T(8,128)(2,1)} %bitcast.7, bf16[1024,8]{0,1:T(8,128)(2,1)S(1)} %bitcast.59, bf16[1024,128]{0,1:T(8,128)(2,1)S(1)} %copy-done.4), kind=kOutput, calls=%fused_computation.11 | convolution fusion | flops 4300210176 | bytes 8667136 | tf_op jit(solution)/shard_map/wq,wmu->mqu/dot_general | solution.py:41
  207.1 6.4 %copy.20 = bf16[8,2048,128]{2,1,0:T(8,128)(2,1)} copy(bf16[8,2048,128]{1,2,0:T(8,128)(2,1)} %fusion.3) | data formatting | bytes 8388608
  213.5 1.5 fusion.15
  215.0 1.2 copy.18
  216.2 7.2 %scatter_custom_fusion = f32[256,512]{1,0:T(8,128)S(1)} fusion(f32[256,512]{1,0:T(8,128)S(1)} %copy.18, s32[1024]{0:T(1024)S(1)} %bitcast.63, bf16[1024,512]{1,0:T(8,128)(2,1)S(1)} %bitcast.52), kind=kCustom, calls=%fused_computation.14 | custom fusion | flops 1048576 | bytes 1572864 | tf_op jit(solution)/shard_map/scatter-add | solution.py:134
  223.4 0.7 convert_element_type.55
  224.1 16.1 %all-to-all-done.4 = bf16[8,128,2048]{2,1,0:T(8,128)(2,1)} async-done(((bf16[8,128,2048]{2,1,0:T(8,128)(2,1)}), bf16[8,128,2048]{2,1,0:T(8,128)(2,1)}, u32[]{:S(2)}, u32[]{:S(2)}) %all-to-all-start.4) | async-done | bytes 4194336 | tf_op jit(solution)/shard_map/all_to_all | solution.py:124
  240.3 17.5 %scatter_custom_fusion.1 = f32[256,2048]{1,0:T(8,128)} fusion(f32[256,2048]{1,0:T(8,128)} %fusion.32, s32[1024]{0:T(1024)S(1)} %bitcast.64, bf16[1024,2048]{1,0:T(8,128)(2,1)} %bitcast.24), kind=kCustom, calls=%fused_computation.5 | custom fusion | flops 4194304 | bytes 6291456 | tf_op jit(solution)/shard_map/scatter-add | solution.py:140
  257.8 2.7 %convert_element_type.60 = bf16[256,2048]{1,0:T(8,128)(2,1)} convert(f32[256,2048]{1,0:T(8,128)} %scatter_custom_fusion.1) | non-fusion elementwise | flops 524288 | bytes 3145728 | tf_op jit(solution)/shard_map/convert_element_type | solution.py:142
  (22 shorter events, 0.5 us)
Async XLA Ops:
  7.2 24.1 %copy-start = (bf16[256,2048]{1,0:T(8,128)(2,1)S(1)}, bf16[256,2048]{1,0:T(8,128)(2,1)}, u32[]{:S(2)}) copy-start(bf16[256,2048]{1,0:T(8,128)(2,1)} %param.7) | copy-start | bytes 3145732
  7.2 14.8 %copy-start.1 = (bf16[256,512]{1,0:T(8,128)(2,1)S(1)}, bf16[256,512]{1,0:T(8,128)(2,1)}, u32[]{:S(2)}) copy-start(bf16[256,512]{1,0:T(8,128)(2,1)} %param.13) | copy-start | bytes 786436
  16.8 10.3 %all-to-all-start.1 = ((bf16[8,128,8]{1,2,0:T(8,128)(2,1)}), bf16[8,128,8]{1,2,0:T(8,128)(2,1)S(1)}, u32[]{:S(2)}, u32[]{:S(2)}) async-start(bf16[8,128,8]{1,2,0:T(8,128)(2,1)} %fusion.27), calls=%async_computation.2 | async-start | bytes 32768 | tf_op jit(solution)/shard_map/all_to_all | solution.py:94
  27.1 19.6 %all-to-all-start.3 = ((bf16[8,128,512]{2,1,0:T(8,128)(2,1)}), bf16[8,128,512]{2,1,0:T(8,128)(2,1)S(1)}, u32[]{:S(2)}, u32[]{:S(2)}) async-start(bf16[8,128,512]{2,1,0:T(8,128)(2,1)} %bitcast.14), calls=%async_computation.4 | async-start | bytes 2097152 | tf_op jit(solution)/shard_map/all_to_all | solution.py:111
  46.7 53.7 %all-to-all-start = ((bf16[8,128,2048]{2,1,0:T(8,128)(2,1)}), bf16[8,128,2048]{2,1,0:T(8,128)(2,1)}, u32[]{:S(2)}, u32[]{:S(2)}) async-start(bf16[8,128,2048]{2,1,0:T(8,128)(2,1)} %bitcast.50), calls=%async_computation.1 | async-start | bytes 8388608 | tf_op jit(solution)/shard_map/all_to_all | solution.py:93
  51.3 140.1 %all-gather.2.cloned.1.call-start = ((), (), s32[]{:S(2)}) async-start(), calls=%async_computation.7 | async-start | bytes 1310720 | tf_op jit(solution)/shard_map/all_gather | solution.py:87
  52.0 7.3 %copy-start.3 = (bf16[8,64,512]{2,1,0:T(8,128)(2,1)S(1)}, bf16[8,64,512]{2,1,0:T(8,128)(2,1)}, u32[]{:S(2)}) copy-start(bf16[8,64,512]{2,1,0:T(8,128)(2,1)} %param.12) | copy-start | bytes 1572868
  52.0 163.0 %reduce-scatter.2.cloned.1.call-start = ((), (), s32[]{:S(2)}) async-start(), calls=%async_computation.6 | async-start | bytes 2621440 | tf_op jit(solution)/shard_map/reduce_scatter | solution.py:77
  167.4 19.0 %all-to-all-start.2 = ((bf16[8,128,512]{2,1,0:T(8,128)(2,1)}), bf16[8,128,512]{2,1,0:T(8,128)(2,1)S(1)}, u32[]{:S(2)}, u32[]{:S(2)}) async-start(bf16[8,128,512]{2,1,0:T(8,128)(2,1)} %bitcast.55), calls=%async_computation.3 | async-start | bytes 2097152 | tf_op jit(solution)/shard_map/all_to_all | solution.py:104
  186.5 4.9 %copy-start.2 = (s32[1,8,128]{2,1,0:T(8,128)S(1)}, s32[1,8,128]{2,1,0:T(8,128)}, u32[]{:S(2)}) copy-start(s32[1,8,128]{2,1,0:T(8,128)} %param.9) | copy-start | bytes 12292
  186.5 53.8 %all-to-all-start.4 = ((bf16[8,128,2048]{2,1,0:T(8,128)(2,1)}), bf16[8,128,2048]{2,1,0:T(8,128)(2,1)}, u32[]{:S(2)}, u32[]{:S(2)}) async-start(bf16[8,128,2048]{2,1,0:T(8,128)(2,1)} %bitcast.51), calls=%async_computation.5 | async-start | bytes 8388608 | tf_op jit(solution)/shard_map/all_to_all | solution.py:124
  191.4 7.5 %copy-start.4 = (bf16[1024,128]{0,1:T(8,128)(2,1)S(1)}, bf16[1024,128]{0,1:T(8,128)(2,1)}, u32[]{:S(2)}) copy-start(bf16[1024,128]{0,1:T(8,128)(2,1)} %get-tuple-element.17) | copy-start | bytes 786436
Sparse Core Ops, SparseCore 0:
  53.7 29.5 all-gather.1
  85.5 58.0 reduce-scatter.1
where the time goes:
time: 268 us; the launch traced here: 267 us
  waiting for transfers between devices  73.5 us (27%)
  blocking collectives  56.5 us (21%)
  matrix products  43.9 us (16%)
  other arithmetic  30.9 us (12%)
  local copies, waits for them, and re-layouts  25.9 us (10%)
  starting transfers between devices  22.5 us (8%)
  between operations  14.2 us (5%)
    psum x1, blocking collectives, shards(): reduced_rank_sum = lax.psum(low_term, 'fsdp')  56.5 us
    all_to_all x1, waiting for transfers between devices, shards(): lax.all_to_all(send_x, 'adapter', split_axis=0, concat_axis=0, tiled=True)  40.2 us
    scatter-add x1, other arithmetic, shards(): adapter_backward = jnp.zeros((rows_here, width_here), jnp.float32).at[dro...  17.5 us
    all_to_all x1, waiting for transfers between devices, shards(): lax.all_to_all(backward_update.reshape(holder_list, slot_capacity, width_...  16.1 us
    all_to_all x1, waiting for transfers between devices, shards(): lax.all_to_all(send_dy, 'adapter', split_axis=0, concat_axis=0, tiled=True)  9.44 us
    dot_general x1, matrix products, backward_owner(): jnp.einsum('wnr,nyr->wy', widened_rows, down_weight, preferred_element_ty...  8.41 us
    dot_general x1, matrix products, backward_owner(): jnp.einsum('wq,wmu->mqu', input_rows, widened_rows, preferred_element_typ...  8.22 us
    dot_general x1, matrix products, down_partial(): jnp.einsum('sd,ldk->slk', input_rows, down_weight, preferred_element_type...  7.56 us
  transfers between devices with their start and end apart: 7, of which 4 were waited for; matrix products, arithmetic and copies ran while one was open for 26% of the time, Pallas kernels for 0%

commit v1 on v0

--- a/solution.py
+++ b/solution.py
@@ -5,6 +5,22 @@
 
 KV = 1024
 adapter_scale = 0.5
+
+
+def exchange_in_pairs(array, axis, split, join):
+    ways, here = (lax.axis_size(axis), lax.axis_index(axis))
+    width = array.shape[split] // ways
+    lengths = list(array.shape)
+    lengths[split] = width
+    height = lengths[join]
+    lengths[join] = height * ways
+    full = jnp.zeros(lengths, array.dtype)
+    for mask in range(ways):
+        part = lax.dynamic_slice_in_dim(array, (here ^ mask) * width, width, axis=split)
+        if mask:
+            part = lax.ppermute(part, axis, [(d, d ^ mask) for d in range(ways)])
+        full = lax.dynamic_update_slice_in_dim(full, part, (here ^ mask) * height, axis=join)
+    return full
 
 
 def down_partial(input_rows, weights_f, down_weight):
@@ -108,7 +124,7 @@
         concat_axis=0,
         tiled=True,
     )
-    recv_dy = lax.all_to_all(send_dy, "adapter", split_axis=0, concat_axis=0, tiled=True)
+    recv_dy = exchange_in_pairs(send_dy, "adapter", 0, 0)
     rows_dy = recv_dy.reshape(total_slots, column_span)
     back_sum = lax.psum(
         grad_partial(rows_dy, weights_f, up_projection_weight, selected_half), "fsdp"

time: 268 us -> 251 us (0.937)
  blocking collectives: 56.5 us -> 45.2 us
  waiting for transfers between devices: 73.5 us -> 63.4 us
  starting transfers between devices: 22.5 us -> 25.3 us
    all_to_all x1, waiting for transfers between devices: 40.2 us -> 0.01 us  [shards(): lax.all_to_all(send_x, 'adapter', split_axis=0, concat_axis=0, tiled=True)]
    ppermute x0 -> x7, waiting for transfers between devices: none -> 39.5 us  [exchange_in_pairs(): part = lax.ppermute(part, axis, [(d, d ^ mask) for d in range(ways)])]
    psum x1, blocking collectives: 56.5 us -> 45.2 us  [shards(): reduced_rank_sum = lax.psum(low_term, 'fsdp')]
    all_to_all x1 -> x0, waiting for transfers between devices: 9.44 us -> none  [shards(): lax.all_to_all(send_dy, 'adapter', split_axis=0, concat_axis=0, tiled=True)]
    ppermute x0 -> x7, starting transfers between devices: none -> 6.93 us  [exchange_in_pairs(): part = lax.ppermute(part, axis, [(d, d ^ mask) for d in range(ways)])]
    all_to_all x1 -> x0, starting transfers between devices: 4.19 us -> none  [shards(): lax.all_to_all(send_dy, 'adapter', split_axis=0, concat_axis=0, tiled=True)]
    unnamed x11 -> x9, local copies, waits for them, and re-layouts: 6.45 us -> 6.44 us
  transfers between devices with their start and end apart: 7 -> 13, of which waited for: 4 -> 6; matrix products, arithmetic and copies ran while one was open for 26% -> 29% of each run, Pallas kernels for 0% -> 0%
where the time goes in v1:
time: 251 us; the launch traced here: 250 us
  waiting for transfers between devices  63.4 us (25%)
  matrix products  45.2 us (18%)
  blocking collectives  45.2 us (18%)
  other arithmetic  30.9 us (12%)
  local copies, waits for them, and re-layouts  25.8 us (10%)
  starting transfers between devices  25.3 us (10%)
  between operations  14.4 us (6%)
    psum x1, blocking collectives, shards(): reduced_rank_sum = lax.psum(low_term, 'fsdp')  45.2 us
    ppermute x7, waiting for transfers between devices, exchange_in_pairs(): part = lax.ppermute(part, axis, [(d, d ^ mask) for d in range(ways)])  39.5 us
    scatter-add x1, other arithmetic, shards(): adapter_backward = jnp.zeros((rows_here, width_here), jnp.float32).at[dro...  17.5 us
    all_to_all x1, waiting for transfers between devices, shards(): lax.all_to_all(backward_update.reshape(holder_list, slot_capacity, width_...  16.3 us
    dot_general x1, matrix products, backward_owner(): jnp.einsum('wnr,nyr->wy', widened_rows, down_weight, preferred_element_ty...  8.44 us
    dot_general x1, matrix products, backward_owner(): jnp.einsum('wq,wmu->mqu', input_rows, widened_rows, preferred_element_typ...  8.23 us
    dot_general x1, matrix products, down_partial(): jnp.einsum('sd,ldk->slk', input_rows, down_weight, preferred_element_type...  7.6 us
    dot_general x1, matrix products, shards(): lax.dot_general(weight_cols, tokens, (((0,), (1,)), ((), ())), preferred_...  7.47 us
  transfers between devices with their start and end apart: 13, of which 6 were waited for; matrix products, arithmetic and copies ran while one was open for 29% of the time, Pallas kernels for 0%

profile of v1, /device:TPU:0, one launch (start us, length us, event | category | flops | bytes accessed | tf_op | source)
XLA Modules:
  0.0 250.2 jit_solution(14656865160020368947)
XLA Ops:
  7.2 0.8 fusion.29
  9.3 6.8 %gather_fusion.1 = s32[1024]{0:T(1024)S(1)} fusion(s32[256]{0:T(256)S(1)} %and_select_fusion, s32[1024]{0:T(1024)S(1)} %fusion.29), kind=kCustom, calls=%fused_computation.1 | custom fusion | bytes 12288 | tf_op jit(solution)/shard_map/gather | solution.py:82
  16.8 5.2 %all-to-all-start.1 = ((bf16[8,128,8]{1,2,0:T(8,128)(2,1)}), bf16[8,128,8]{1,2,0:T(8,128)(2,1)S(1)}, u32[]{:S(2)}, u32[]{:S(2)}) async-start(bf16[8,128,8]{1,2,0:T(8,128)(2,1)} %fusion.27), calls=%async_computation.2 | async-start | bytes 32768 | tf_op jit(solution)/shard_map/all_to_all | solution.py:110
  22.0 6.0 %gather_fusion = bf16[1024,2048]{1,0:T(8,128)(2,1)} fusion(bf16[256,2048]{1,0:T(8,128)(2,1)S(1)} %copy-done, s32[1024]{0:T(1024)S(1)} %fusion.29), kind=kCustom, calls=%fused_computation | custom fusion | bytes 8392704 | tf_op jit(solution)/shard_map/gather | solution.py:87
  27.9 4.7 %all-to-all-start = ((bf16[8,128,2048]{2,1,0:T(8,128)(2,1)}), bf16[8,128,2048]{2,1,0:T(8,128)(2,1)}, u32[]{:S(2)}, u32[]{:S(2)}) async-start(bf16[8,128,2048]{2,1,0:T(8,128)(2,1)} %bitcast.50), calls=%async_computation.1 | async-start | bytes 8388608 | tf_op jit(solution)/shard_map/all_to_all | solution.py:109
  33.5 4.0 %gather_fusion.2 = bf16[1024,512]{1,0:T(8,128)(2,1)S(1)} fusion(bf16[256,512]{1,0:T(8,128)(2,1)S(1)} %copy-done.1, s32[1024]{0:T(1024)S(1)} %fusion.29), kind=kCustom, calls=%fused_computation.2 | custom fusion | bytes 2101248 | tf_op jit(solution)/shard_map/gather | solution.py:88
  37.6 0.8 constant_dynamic-slice_fusion
  38.8 1.7 collective-permute-start.1
  40.6 1.7 collective-permute-start.3
  42.3 7.5 %fusion.31 = f32[2048,256]{1,0:T(8,128)} fusion(bf16[2048,2048]{1,0:T(8,128)(2,1)} %param.10, bf16[256,2048]{1,0:T(8,128)(2,1)S(1)} %copy-done), kind=kOutput, calls=%fused_computation.64 | convolution fusion | flops 2147483648 | bytes 11534336 | tf_op jit(solution)/shard_map/dot_general | solution.py:94
  49.9 2.7 %collective-permute-start.5 = (bf16[1,128,512]{2,1,0:T(8,128)(2,1)S(1)}, bf16[1,128,512]{2,1,0:T(8,128)(2,1)S(1)}, u32[]{:S(2)}, u32[]{:S(2)}) collective-permute-start(bf16[1,128,512]{2,1,0:T(8,128)(2,1)S(1)} %get-tuple-element.19), channel_id=1, source_target_pairs={{0,6},{1,7},{2,4},{3,5},{4,2},{5,3},{6,0},{7,1},{8,14},{9,15},{10,... | collective-permute-start | bytes 393224 | tf_op jit(solution)/shard_map/ppermute | solution.py:21
  52.6 31.5 %collective-permute-done.1 = bf16[1,128,512]{2,1,0:T(8,128)(2,1)S(1)} collective-permute-done((bf16[1,128,512]{2,1,0:T(8,128)(2,1)}, bf16[1,128,512]{2,1,0:T(8,128)(2,1)S(1)}, u32[]{:S(2)}, u32[]{:S(2)}) %collective-permute-start.1) | collective-permute-done | bytes 131104 | tf_op jit(solution)/shard_map/ppermute | solution.py:21
  84.4 1.5 collective-permute-done.2
  86.0 4.6 %collective-permute-done.5 = bf16[1,128,512]{2,1,0:T(8,128)(2,1)S(1)} collective-permute-done((bf16[1,128,512]{2,1,0:T(8,128)(2,1)S(1)}, bf16[1,128,512]{2,1,0:T(8,128)(2,1)S(1)}, u32[]{:S(2)}, u32[]{:S(2)}) %collective-permute-start.5) | collective-permute-done | bytes 131104 | tf_op jit(solution)/shard_map/ppermute | solution.py:21
  90.6 1.8 collective-permute-done.6
  92.5 1.8 multiply_reduce_fusion.1
  94.4 7.6 %multiply_reduce_fusion = f32[1024,128]{1,0:T(8,128)S(1)} fusion(bf16[1024,2048,1]{1,0,2:T(8,128)(2,1)} %bitcast.7, bf16[8,2048,128]{2,1,0:T(8,128)(2,1)} %param.11, f32[1024,8]{0,1:T(8,128)S(1)} %bitcast_convert_fusion), kind=kOutput, calls=%fused_computation.10 | convolution fusion | flops 4296933376 | bytes 8945664 | tf_op jit(solution)/shard_map/sd,ldk->slk/dot_general | solution.py:27
  102.0 45.2 %all-reduce.2 = (bf16[1024,128]{1,0:T(8,128)(2,1)S(1)}, bf16[1024,128]{0,1:T(8,128)(2,1)}) all-reduce(f32[1024,128]{1,0:T(8,128)S(1)} %multiply_reduce_fusion, f32[1024,128]{0,1:T(8,128)S(1)} %constant_dynamic-update-slice_fusion.7), channel_id=1, replica_groups=mesh['fsdp'=4,'adapter'=8] {'fsdp'}, use_global_device_ids=true, to_apply=%region_2.3 | all-reduce | flops 262144 | bytes 1572864 | tf_op jit(solution)/shard_map/psum | solution.py:116
  147.5 2.8 %fusion.8 = bf16[1024,512]{1,0:T(8,128)(2,1)} fusion(bf16[8,64,512]{2,1,0:T(8,128)(2,1)} %param.12, bf16[1024,8]{0,1:T(8,128)(2,1)S(1)} %bitcast.58, bf16[1024,64]{0,1:T(8,128)(2,1)S(1)} %copy.17), kind=kOutput, calls=%fused_computation.17 | convolution fusion | flops 538443776 | bytes 1720320 | tf_op jit(solution)/shard_map/slr,lrc->sc/dot_general | solution.py:46
  150.2 3.6 %all-to-all-start.2 = ((bf16[8,128,512]{2,1,0:T(8,128)(2,1)}), bf16[8,128,512]{2,1,0:T(8,128)(2,1)S(1)}, u32[]{:S(2)}, u32[]{:S(2)}) async-start(bf16[8,128,512]{2,1,0:T(8,128)(2,1)} %bitcast.56), calls=%async_computation.3 | async-start | bytes 2097152 | tf_op jit(solution)/shard_map/all_to_all | solution.py:120
  153.8 8.4 %fusion.2 = bf16[1024,2048]{1,0:T(8,128)(2,1)} fusion(bf16[8,2048,128]{2,1,0:T(8,128)(2,1)} %param.11, bf16[1024,8]{0,1:T(8,128)(2,1)S(1)} %bitcast.59, bf16[1024,128]{0,1:T(8,128)(2,1)} %get-tuple-element.17), kind=kOutput, calls=%fused_computation.8 | convolution fusion | flops 4300210176 | bytes 8667136 | tf_op jit(solution)/shard_map/wnr,nyr->wy/dot_general | solution.py:54
  162.2 6.9 %all-to-all-done.2 = bf16[8,128,512]{2,1,0:T(8,128)(2,1)S(1)} async-done(((bf16[8,128,512]{2,1,0:T(8,128)(2,1)}), bf16[8,128,512]{2,1,0:T(8,128)(2,1)S(1)}, u32[]{:S(2)}, u32[]{:S(2)}) %all-to-all-start.2) | async-done | bytes 1048608 | tf_op jit(solution)/shard_map/all_to_all | solution.py:120
  169.1 4.9 %all-to-all-start.3 = ((bf16[8,128,2048]{2,1,0:T(8,128)(2,1)}), bf16[8,128,2048]{2,1,0:T(8,128)(2,1)}, u32[]{:S(2)}, u32[]{:S(2)}) async-start(bf16[8,128,2048]{2,1,0:T(8,128)(2,1)} %bitcast.52), calls=%async_computation.4 | async-start | bytes 8388608 | tf_op jit(solution)/shard_map/all_to_all | solution.py:140
  174.1 7.4 %fusion.32 = f32[256,2048]{1,0:T(8,128)} fusion(bf16[256,2048]{1,0:T(8,128)(2,1)} %all-gather.2.cloned.1.call-done, bf16[2048,2048]{1,0:T(8,128)(2,1)} %param.10), kind=kOutput, calls=%fused_computation.65 | convolution fusion | flops 2147483648 | bytes 11534336 | tf_op jit(solution)/shard_map/dot_general | solution.py:102
  181.5 8.2 %fusion.3 = bf16[8,2048,128]{1,2,0:T(8,128)(2,1)} fusion(bf16[1024,2048,1]{1,0,2:T(8,128)(2,1)} %bitcast.7, bf16[1024,8]{0,1:T(8,128)(2,1)S(1)} %bitcast.60, bf16[1024,128]{0,1:T(8,128)(2,1)S(1)} %copy-done.3), kind=kOutput, calls=%fused_computation.11 | convolution fusion | flops 4300210176 | bytes 8667136 | tf_op jit(solution)/shard_map/wq,wmu->mqu/dot_general | solution.py:57
  189.7 6.4 %copy.20 = bf16[8,2048,128]{2,1,0:T(8,128)(2,1)} copy(bf16[8,2048,128]{1,2,0:T(8,128)(2,1)} %fusion.3) | data formatting | bytes 8388608
  196.2 1.5 fusion.15
  197.7 1.2 copy.18
  198.9 7.2 %scatter_custom_fusion = f32[256,512]{1,0:T(8,128)S(1)} fusion(f32[256,512]{1,0:T(8,128)S(1)} %copy.18, s32[1024]{0:T(1024)S(1)} %bitcast.64, bf16[1024,512]{1,0:T(8,128)(2,1)S(1)} %bitcast.53), kind=kCustom, calls=%fused_computation.14 | custom fusion | flops 1048576 | bytes 1572864 | tf_op jit(solution)/shard_map/scatter-add | solution.py:150
  206.8 16.3 %all-to-all-done.3 = bf16[8,128,2048]{2,1,0:T(8,128)(2,1)} async-done(((bf16[8,128,2048]{2,1,0:T(8,128)(2,1)}), bf16[8,128,2048]{2,1,0:T(8,128)(2,1)}, u32[]{:S(2)}, u32[]{:S(2)}) %all-to-all-start.3) | async-done | bytes 4194336 | tf_op jit(solution)/shard_map/all_to_all | solution.py:140
  223.1 17.5 %scatter_custom_fusion.1 = f32[256,2048]{1,0:T(8,128)} fusion(f32[256,2048]{1,0:T(8,128)} %fusion.32, s32[1024]{0:T(1024)S(1)} %bitcast.65, bf16[1024,2048]{1,0:T(8,128)(2,1)} %bitcast.24), kind=kCustom, calls=%fused_computation.5 | custom fusion | flops 4194304 | bytes 6291456 | tf_op jit(solution)/shard_map/scatter-add | solution.py:156
  240.6 2.7 %convert_element_type.60 = bf16[256,2048]{1,0:T(8,128)(2,1)} convert(f32[256,2048]{1,0:T(8,128)} %scatter_custom_fusion.1) | non-fusion elementwise | flops 524288 | bytes 3145728 | tf_op jit(solution)/shard_map/convert_element_type | solution.py:158
  (41 shorter events, 5.0 us)
Async XLA Ops:
  7.2 14.8 %copy-start = (bf16[256,2048]{1,0:T(8,128)(2,1)S(1)}, bf16[256,2048]{1,0:T(8,128)(2,1)}, u32[]{:S(2)}) copy-start(bf16[256,2048]{1,0:T(8,128)(2,1)} %param.7) | copy-start | bytes 3145732
  16.8 11.1 %all-to-all-start.1 = ((bf16[8,128,8]{1,2,0:T(8,128)(2,1)}), bf16[8,128,8]{1,2,0:T(8,128)(2,1)S(1)}, u32[]{:S(2)}, u32[]{:S(2)}) async-start(bf16[8,128,8]{1,2,0:T(8,128)(2,1)} %fusion.27), calls=%async_computation.2 | async-start | bytes 32768 | tf_op jit(solution)/shard_map/all_to_all | solution.py:110
  27.9 5.5 %copy-start.1 = (bf16[256,512]{1,0:T(8,128)(2,1)S(1)}, bf16[256,512]{1,0:T(8,128)(2,1)}, u32[]{:S(2)}) copy-start(bf16[256,512]{1,0:T(8,128)(2,1)} %param.13) | copy-start | bytes 786436
  27.9 66.4 %all-to-all-start = ((bf16[8,128,2048]{2,1,0:T(8,128)(2,1)}), bf16[8,128,2048]{2,1,0:T(8,128)(2,1)}, u32[]{:S(2)}, u32[]{:S(2)}) async-start(bf16[8,128,2048]{2,1,0:T(8,128)(2,1)} %bitcast.50), calls=%async_computation.1 | async-start | bytes 8388608 | tf_op jit(solution)/shard_map/all_to_all | solution.py:109
  32.6 141.4 %all-gather.2.cloned.1.call-start = ((), (), s32[]{:S(2)}) async-start(), calls=%async_computation.6 | async-start | bytes 1310720 | tf_op jit(solution)/shard_map/all_gather | solution.py:103
  33.4 164.3 %reduce-scatter.2.cloned.1.call-start = ((), (), s32[]{:S(2)}) async-start(), calls=%async_computation.5 | async-start | bytes 2621440 | tf_op jit(solution)/shard_map/reduce_scatter | solution.py:93
  38.4 11.5 %collective-permute-start = (bf16[1,128,512]{2,1,0:T(8,128)(2,1)}, bf16[1,128,512]{2,1,0:T(8,128)(2,1)S(1)}, u32[]{:S(2)}, u32[]{:S(2)}) collective-permute-start(bf16[1,128,512]{2,1,0:T(8,128)(2,1)} %get-tuple-element.24), channel_id=1, source_target_pairs={{0,1},{1,0},{2,3},{3,2},{4,5},{5,4},{6,7},{7,6},{8,9},{9,8},{10,11... | collective-permute-start | bytes 393224 | tf_op jit(solution)/shard_map/ppermute | solution.py:21
  38.8 45.2 %collective-permute-start.1 = (bf16[1,128,512]{2,1,0:T(8,128)(2,1)}, bf16[1,128,512]{2,1,0:T(8,128)(2,1)S(1)}, u32[]{:S(2)}, u32[]{:S(2)}) collective-permute-start(bf16[1,128,512]{2,1,0:T(8,128)(2,1)} %get-tuple-element.23), channel_id=1, source_target_pairs={{0,2},{1,3},{2,0},{3,1},{4,6},{5,7},{6,4},{7,5},{8,10},{9,11},{10,... | collective-permute-start | bytes 393224 | tf_op jit(solution)/shard_map/ppermute | solution.py:21
  40.5 45.4 %collective-permute-start.2 = (bf16[1,128,512]{2,1,0:T(8,128)(2,1)}, bf16[1,128,512]{2,1,0:T(8,128)(2,1)S(1)}, u32[]{:S(2)}, u32[]{:S(2)}) collective-permute-start(bf16[1,128,512]{2,1,0:T(8,128)(2,1)} %get-tuple-element.22), channel_id=1, source_target_pairs={{0,3},{1,2},{2,1},{3,0},{4,7},{5,6},{6,5},{7,4},{8,11},{9,10},{10,... | collective-permute-start | bytes 393224 | tf_op jit(solution)/shard_map/ppermute | solution.py:21
  40.6 45.4 %collective-permute-start.3 = (bf16[1,128,512]{2,1,0:T(8,128)(2,1)}, bf16[1,128,512]{2,1,0:T(8,128)(2,1)S(1)}, u32[]{:S(2)}, u32[]{:S(2)}) collective-permute-start(bf16[1,128,512]{2,1,0:T(8,128)(2,1)} %get-tuple-element.21), channel_id=1, source_target_pairs={{0,4},{1,5},{2,6},{3,7},{4,0},{5,1},{6,2},{7,3},{8,12},{9,13},{10,... | collective-permute-start | bytes 393224 | tf_op jit(solution)/shard_map/ppermute | solution.py:21
  42.2 43.7 %collective-permute-start.4 = (bf16[1,128,512]{2,1,0:T(8,128)(2,1)S(1)}, bf16[1,128,512]{2,1,0:T(8,128)(2,1)S(1)}, u32[]{:S(2)}, u32[]{:S(2)}) collective-permute-start(bf16[1,128,512]{2,1,0:T(8,128)(2,1)S(1)} %get-tuple-element.20), channel_id=1, source_target_pairs={{0,5},{1,4},{2,7},{3,6},{4,1},{5,0},{6,3},{7,2},{8,13},{9,12},{10,... | collective-permute-start | bytes 393224 | tf_op jit(solution)/shard_map/ppermute | solution.py:21
  49.9 40.7 %collective-permute-start.5 = (bf16[1,128,512]{2,1,0:T(8,128)(2,1)S(1)}, bf16[1,128,512]{2,1,0:T(8,128)(2,1)S(1)}, u32[]{:S(2)}, u32[]{:S(2)}) collective-permute-start(bf16[1,128,512]{2,1,0:T(8,128)(2,1)S(1)} %get-tuple-element.19), channel_id=1, source_target_pairs={{0,6},{1,7},{2,4},{3,5},{4,2},{5,3},{6,0},{7,1},{8,14},{9,15},{10,... | collective-permute-start | bytes 393224 | tf_op jit(solution)/shard_map/ppermute | solution.py:21
  84.1 8.4 %collective-permute-start.6 = (bf16[1,128,512]{2,1,0:T(8,128)(2,1)S(1)}, bf16[1,128,512]{2,1,0:T(8,128)(2,1)S(1)}, u32[]{:S(2)}, u32[]{:S(2)}) collective-permute-start(bf16[1,128,512]{2,1,0:T(8,128)(2,1)S(1)} %get-tuple-element.18), channel_id=1, source_target_pairs={{0,7},{1,6},{2,5},{3,4},{4,3},{5,2},{6,1},{7,0},{8,15},{9,14},{10,... | collective-permute-start | bytes 393224 | tf_op jit(solution)/shard_map/ppermute | solution.py:21
  150.2 18.9 %all-to-all-start.2 = ((bf16[8,128,512]{2,1,0:T(8,128)(2,1)}), bf16[8,128,512]{2,1,0:T(8,128)(2,1)S(1)}, u32[]{:S(2)}, u32[]{:S(2)}) async-start(bf16[8,128,512]{2,1,0:T(8,128)(2,1)} %bitcast.56), calls=%async_computation.3 | async-start | bytes 2097152 | tf_op jit(solution)/shard_map/all_to_all | solution.py:120
  169.1 4.9 %copy-start.2 = (s32[1,8,128]{2,1,0:T(8,128)S(1)}, s32[1,8,128]{2,1,0:T(8,128)}, u32[]{:S(2)}) copy-start(s32[1,8,128]{2,1,0:T(8,128)} %param.9) | copy-start | bytes 12292
  169.1 54.0 %all-to-all-start.3 = ((bf16[8,128,2048]{2,1,0:T(8,128)(2,1)}), bf16[8,128,2048]{2,1,0:T(8,128)(2,1)}, u32[]{:S(2)}, u32[]{:S(2)}) async-start(bf16[8,128,2048]{2,1,0:T(8,128)(2,1)} %bitcast.52), calls=%async_computation.4 | async-start | bytes 8388608 | tf_op jit(solution)/shard_map/all_to_all | solution.py:140
  174.1 7.4 %copy-start.3 = (bf16[1024,128]{0,1:T(8,128)(2,1)S(1)}, bf16[1024,128]{0,1:T(8,128)(2,1)}, u32[]{:S(2)}) copy-start(bf16[1024,128]{0,1:T(8,128)(2,1)} %get-tuple-element.17) | copy-start | bytes 786436
Sparse Core Ops, SparseCore 0:
  35.0 29.5 all-gather.1
  67.0 43.4 reduce-scatter.1
